TPU v7x, 128 devices: a whole 4x4x4 slice. The times are simulated.
128 devices in a mesh: row: 8 (over y, core), col: 16 (over x, z).
Axes of the slice: x: 4, y: 4, z: 4, core: 2. Of those that a mesh axis runs over, the one named last changes fastest.
Arguments:
- points: bfloat16 [1048576, 768], P(('row', 'col')), may hold values from -6 to 6
- node_of_row: int32 [1048576], P(('row', 'col')), may hold values from 0 to 255, as said below
- init_axes: float32 [768, 8], replicated, may hold values from -0.21875 to 0.21875
Outputs:
- projected: float32 [8, 1048576], P(None, ('row', 'col'))
Inputs may be any that keep to these rules, and one draw needn't show every extreme that they name: `node_of_row`: never falls along the points; every one of the 256 nodes has at least 512 points; the points of one device belong to at most 8 nodes, and exactly 8 on some device; a node may cover many devices.
All inputs are finite; a program needn't handle non-finite values.
Results may differ from a plain program's by a relative error of at most 0.0035.
The roundings to bfloat16 on the way count: a program that leaves them out, or rounds other values in their place, can miss the bound.
Values sent between devices are 32-bit elements; how exact they have to be, the bound alone decides.
A program may use at most 128 MiB of HBM per device.

v0:
```python
import jax
import jax.numpy as jnp
from jax import lax
from jax.sharding import Mesh
from jax.sharding import PartitionSpec as P

AXES = 8
ITERS = 3
SPAN_MOST = 8
ROW_COL = ("row_0", "row_1", "col_0", "col_1")


def laid_out(blocks, dim):
    dims = list(blocks.shape[1:])
    dims[dim] *= blocks.shape[0]
    return jnp.moveaxis(blocks, 0, dim).reshape(dims)


def gather_in_order(value, axes, order):
    blocks = value[None]
    for k in order:
        blocks = lax.all_gather(blocks, axes[k], axis=0, tiled=True)
    block = [lax.axis_size(axes[k]) for k in reversed(order)]
    blocks = blocks.reshape(*block, *value.shape)
    turned = sorted(range(len(order)), key=lambda place: order[len(order) - 1 - place])
    return blocks.transpose(*turned, *range(len(order), blocks.ndim)).reshape(-1, *value.shape)


def whole_of(value, axes, order, dim):
    return laid_out(gather_in_order(value, axes, order), dim)


def orthonormal(moment):
    found = []
    for index in range(moment.shape[1]):
        vector = moment[:, index]
        for column in found:
            vector = vector - jnp.sum(column * vector) * column
        vector = vector / jnp.sqrt(jnp.sum(vector * vector))
        found.append(vector)
    return jnp.stack(found, 1)


def lifted_terms(block, frames, centre):
    offset = jnp.einsum("ld,ldk->lk", centre, frames, precision=lax.Precision.HIGHEST)
    flat_frames = frames.astype(jnp.bfloat16).transpose(1, 0, 2).reshape(frames.shape[1], -1)
    spread = jnp.dot(block, flat_frames, preferred_element_type=jnp.float32)
    return spread.reshape(block.shape[0], SPAN_MOST, AXES) - offset[None]


def local_moment(block, member, frames, centre):
    terms = lifted_terms(block, frames, centre)
    lifted = terms.astype(jnp.bfloat16) * member.astype(jnp.bfloat16)[:, :, None]
    moment = lax.dot_general(
        block,
        lifted.reshape(block.shape[0], -1),
        (((0,), (0,)), ((), ())),
        preferred_element_type=jnp.float32,
    )
    moment = moment.reshape(block.shape[1], SPAN_MOST, AXES).transpose(1, 0, 2)
    column_sums = jnp.sum(lifted.astype(jnp.float32), 0)
    return moment - centre[:, :, None] * column_sums[:, None, :]


def settle(pieces, first_node, last_node):
    span_count = last_node - first_node
    first_mark = first_node.astype(jnp.float32)
    last_mark = last_node.astype(jnp.float32)
    flat_parts = [piece.reshape(piece.shape[0], -1) for piece in pieces]
    head_rows = tuple((flat[0:1] for flat in flat_parts))
    tail_rows = tuple((lax.dynamic_slice_in_dim(flat, span_count, 1, 0) for flat in flat_parts))
    tail_only = tuple((jnp.where(span_count > 0, tail, 0.0) for tail in tail_rows))
    node_marks = jnp.stack([first_mark, last_mark]).reshape(1, 2)
    gathered = jax.tree.map(
        lambda part: whole_of(part, ROW_COL, (0, 2, 3, 1), 0), (node_marks,) + head_rows + tail_only
    )
    marks_all = gathered[0]
    count_parts = len(flat_parts)
    not_self = jnp.arange(marks_all.shape[0], dtype=jnp.int32) != lax.axis_index(ROW_COL)
    head_first = (not_self & (marks_all[:, 0] == first_mark))[:, None]
    tail_first = (not_self & (marks_all[:, 1] == first_mark))[:, None]
    head_last = (not_self & (marks_all[:, 0] == last_mark) & (last_node != first_node))[:, None]
    tail_last = (not_self & (marks_all[:, 1] == last_mark) & (last_node != first_node))[:, None]
    into_first = []
    into_last = []
    for index in range(count_parts):
        heads_all = gathered[1 + index]
        tails_all = gathered[1 + count_parts + index]
        into_first.append(
            jnp.sum(
                jnp.where(head_first, heads_all, 0.0) + jnp.where(tail_first, tails_all, 0.0),
                0,
                keepdims=True,
            )
        )
        into_last.append(
            jnp.sum(
                jnp.where(head_last, heads_all, 0.0) + jnp.where(tail_last, tails_all, 0.0),
                0,
                keepdims=True,
            )
        )
    slot_index = jnp.arange(SPAN_MOST, dtype=jnp.int32)[:, None]
    settled = []
    for piece, flat, add_first, add_last in zip(pieces, flat_parts, into_first, into_last):
        whole = (
            flat
            + jnp.where(slot_index == 0, add_first, 0.0)
            + jnp.where(slot_index == span_count, add_last, 0.0)
        )
        settled.append(whole.reshape(piece.shape))
    return settled


def shards(points, node_of_row, init_axes):
    row_count = points.shape[0]
    width = points.shape[1]
    first_node = node_of_row[0]
    last_node = node_of_row[-1]
    slot_index = jnp.arange(SPAN_MOST, dtype=jnp.int32)
    member = (node_of_row[:, None] - first_node == slot_index[None, :]).astype(jnp.float32)
    node_sums = lax.dot_general(
        member.astype(jnp.bfloat16),
        points,
        (((0,), (0,)), ((), ())),
        preferred_element_type=jnp.float32,
    )
    node_counts = jnp.sum(member, 0)
    node_sums, node_counts = settle([node_sums, node_counts], first_node, last_node)
    live_slot = slot_index <= last_node - first_node
    centre = node_sums / jnp.where(live_slot, node_counts, 1.0)[:, None]
    start_frames = jnp.broadcast_to(init_axes, (SPAN_MOST, width, AXES))
    frames = start_frames
    for repeat in range(ITERS):
        moment = local_moment(points, member, frames, centre)
        (moment,) = settle([moment], first_node, last_node)
        moment = jnp.where(live_slot[:, None, None], moment, start_frames)
        frames = jax.vmap(orthonormal)(moment)
    terms = lifted_terms(points, frames, centre)
    coords = jnp.sum(terms * member[:, :, None], 1)
    return coords.reshape(row_count, AXES).T


def solution(mesh):
    split = Mesh(mesh.devices.reshape(4, 2, 4, 4), ("row_0", "row_1", "col_0", "col_1"))
    return jax.shard_map(
        shards,
        mesh=split,
        in_specs=(P(ROW_COL, None), P(ROW_COL), P()),
        out_specs=P(None, ROW_COL),
        check_vma=False,
    )
```

profile of v0, /device:TPU:1, one launch (start us, length us, event | category | flops | bytes accessed | tf_op | source)
XLA Modules:
  0.0 663.2 jit_solution(4486327910379594088)
XLA Ops:
  36.8 10.2 %all_gather.146 = f32[64,1,2]{2,1,0:T(1,128)S(1)} all-gather(f32[16,1,2]{2,1,0:T(1,128)S(1)} %all_gather.145), channel_id=1, replica_groups=mesh['row_0'=4,'row_1'=2,'col_0'=4,'col_1'=4] {'col_1'}, dimensions={0}, use_global_device_ids=true | all-gather | bytes 640 | tf_op jit(solution)/shard_map/all_gather | solution.py:22
  121.5 10.4 %all-gather.8 = f32[128,768]{1,0:T(8,128)S(1)} all-gather(f32[64,768]{1,0:T(8,128)S(1)} %all-gather.7), channel_id=10, replica_groups=mesh['row_0'=4,'row_1'=2,'col_0'=4,'col_1'=4] {'row_1'}, dimensions={0}, use_global_device_ids=true | all-gather | bytes 589824 | tf_op jit(solution)/shard_map/all_gather | solution.py:22
  159.6 10.6 %all-gather.4 = f32[128,768]{1,0:T(8,128)S(1)} all-gather(f32[64,768]{1,0:T(8,128)S(1)} %all-gather.3), channel_id=6, replica_groups=mesh['row_0'=4,'row_1'=2,'col_0'=4,'col_1'=4] {'row_1'}, dimensions={0}, use_global_device_ids=true | all-gather | bytes 589824 | tf_op jit(solution)/shard_map/all_gather | solution.py:22
  202.4 10.8 %all-gather.34 = f32[4,4,6144]{2,1,0:T(4,128)S(1)} all-gather(f32[1,4,6144]{2,1,0:T(4,128)S(1)} %copy.263), channel_id=20, replica_groups=mesh['row_0'=4,'row_1'=2,'col_0'=4,'col_1'=4] {'col_0'}, dimensions={0}, use_global_device_ids=true | all-gather | bytes 491520 | tf_op jit(solution)/shard_map/all_gather | solution.py:22
  223.7 10.9 %all_gather.165 = f32[16,1,6144]{2,1,0:T(1,128)} all-gather(f32[4,1,6144]{2,1,0:T(1,128)S(1)} %all_gather.164), channel_id=1, replica_groups=mesh['row_0'=4,'row_1'=2,'col_0'=4,'col_1'=4] {'col_0'}, dimensions={0}, use_global_device_ids=true | all-gather | bytes 491520 | tf_op jit(solution)/shard_map/all_gather | solution.py:22
  241.7 28.1 %all-gather.52.cloned.1.call-done = f32[64,1,6144]{2,1,0:T(1,128)} async-done(((f32[16,1,6144]{2,1,0:T(1,128)}), f32[64,1,6144]{2,1,0:T(1,128)}) %all-gather.52.cloned.1.call-update) | async-done | bytes 1572880 | tf_op jit(solution)/shard_map/all_gather | solution.py:22
  270.7 16.0 %all-gather.66.cloned.1.call-done = f32[128,6144]{1,0:T(8,128)} async-done(((f32[64,6144]{1,0:T(8,128)}), f32[128,6144]{1,0:T(8,128)}) %all-gather.66.cloned.1.call-update) | async-done | bytes 3145744 | tf_op jit(solution)/shard_map/all_gather | solution.py:22
  291.9 12.6 %all-gather.54.cloned.1.call-done = f32[128,1,6144]{2,1,0:T(1,128)} async-done(((f32[64,1,6144]{2,1,0:T(1,128)}), f32[128,1,6144]{2,1,0:T(1,128)}) %all-gather.54.cloned.1.call-update) | async-done | bytes 3145744 | tf_op jit(solution)/shard_map/all_gather | solution.py:22
  304.4 15.6 %fusion.30 = (f32[6144]{0:T(1024)}, f32[6144]{0:T(1024)}) fusion(f32[2,4,4,4,1,6144]{5,4,3,2,1,0:T(1,128)S(1)} %reshape.2690, pred[4,2,4,4]{0,2,3,1:T(4,128)(4,1)S(1)} %copy.251, f32[4,2,4,4,1,6144]{5,4,0,2,3,1:T(1,128)} %bitcast.468, pred[4,2,4,4]{0,2,3,1:T(4,128)(4,1)S(1)} %copy.249, pred[4,2,4,4]{0,2,3,1:T(4,128)(4,1)S(1)} %copy-done.6, ...), kind=kLoop, calls=%fused_computation.39 | loop fusion | flops 6279168 | bytes 6341120 | tf_op jit(solution)/shard_map/reduce_sum | solution.py:90
  350.3 9.9 %all-gather.35 = f32[4,1,6144]{2,1,0:T(1,128)S(1)} all-gather(f32[1,1,6144]{2,1,0:T(1,128)S(1)} %fusion.57), channel_id=23, replica_groups=mesh['row_0'=4,'row_1'=2,'col_0'=4,'col_1'=4] {'row_0'}, dimensions={0}, use_global_device_ids=true | all-gather | bytes 122880 | tf_op jit(solution)/shard_map/all_gather | solution.py:22
  360.2 10.0 %all-gather.36 = f32[4,4,6144]{2,1,0:T(4,128)S(1)} all-gather(f32[1,4,6144]{2,1,0:T(4,128)S(1)} %copy.274), channel_id=24, replica_groups=mesh['row_0'=4,'row_1'=2,'col_0'=4,'col_1'=4] {'col_0'}, dimensions={0}, use_global_device_ids=true | all-gather | bytes 491520 | tf_op jit(solution)/shard_map/all_gather | solution.py:22
  380.6 11.5 %all_gather.173 = f32[16,1,6144]{2,1,0:T(1,128)} all-gather(f32[4,1,6144]{2,1,0:T(1,128)S(1)} %all_gather.172), channel_id=1, replica_groups=mesh['row_0'=4,'row_1'=2,'col_0'=4,'col_1'=4] {'col_0'}, dimensions={0}, use_global_device_ids=true | all-gather | bytes 491520 | tf_op jit(solution)/shard_map/all_gather | solution.py:22
  392.1 10.7 %all-gather.68.cloned.1.call-done = f32[64,6144]{1,0:T(8,128)} async-done(((f32[16,6144]{1,0:T(8,128)}), f32[64,6144]{1,0:T(8,128)}) %all-gather.68.cloned.1.call-update) | async-done | bytes 1572880 | tf_op jit(solution)/shard_map/all_gather | solution.py:22
  402.9 28.0 %all-gather.56.cloned.1.call-done = f32[64,1,6144]{2,1,0:T(1,128)} async-done(((f32[16,1,6144]{2,1,0:T(1,128)}), f32[64,1,6144]{2,1,0:T(1,128)}) %all-gather.56.cloned.1.call-update) | async-done | bytes 1572880 | tf_op jit(solution)/shard_map/all_gather | solution.py:22
  431.0 16.8 %all-gather.70.cloned.1.call-done = f32[128,6144]{1,0:T(8,128)} async-done(((f32[64,6144]{1,0:T(8,128)}), f32[128,6144]{1,0:T(8,128)}) %all-gather.70.cloned.1.call-update) | async-done | bytes 3145744 | tf_op jit(solution)/shard_map/all_gather | solution.py:22
  452.9 12.7 %all-gather.58.cloned.1.call-done = f32[128,1,6144]{2,1,0:T(1,128)} async-done(((f32[64,1,6144]{2,1,0:T(1,128)}), f32[128,1,6144]{2,1,0:T(1,128)}) %all-gather.58.cloned.1.call-update) | async-done | bytes 3145744 | tf_op jit(solution)/shard_map/all_gather | solution.py:22
  465.6 15.6 %fusion.29 = (f32[6144]{0:T(1024)}, f32[6144]{0:T(1024)}) fusion(f32[2,4,4,4,1,6144]{5,4,3,2,1,0:T(1,128)S(1)} %reshape.2691, pred[4,2,4,4]{0,2,3,1:T(4,128)(4,1)S(1)} %copy.251, f32[4,2,4,4,1,6144]{5,4,0,2,3,1:T(1,128)} %bitcast.470, pred[4,2,4,4]{0,2,3,1:T(4,128)(4,1)S(1)} %copy.249, pred[4,2,4,4]{0,2,3,1:T(4,128)(4,1)S(1)} %copy-done.7, ...), kind=kLoop, calls=%fused_computation.38 | loop fusion | flops 6279168 | bytes 6341120 | tf_op jit(solution)/shard_map/reduce_sum | solution.py:90
  521.1 10.0 %all-gather.38 = f32[4,4,6144]{2,1,0:T(4,128)S(1)} all-gather(f32[1,4,6144]{2,1,0:T(4,128)S(1)} %copy.283), channel_id=28, replica_groups=mesh['row_0'=4,'row_1'=2,'col_0'=4,'col_1'=4] {'col_0'}, dimensions={0}, use_global_device_ids=true | all-gather | bytes 491520 | tf_op jit(solution)/shard_map/all_gather | solution.py:22
  541.5 11.5 %all_gather.181 = f32[16,1,6144]{2,1,0:T(1,128)} all-gather(f32[4,1,6144]{2,1,0:T(1,128)S(1)} %all_gather.180), channel_id=1, replica_groups=mesh['row_0'=4,'row_1'=2,'col_0'=4,'col_1'=4] {'col_0'}, dimensions={0}, use_global_device_ids=true | all-gather | bytes 491520 | tf_op jit(solution)/shard_map/all_gather | solution.py:22
  553.1 10.7 %all-gather.72.cloned.1.call-done = f32[64,6144]{1,0:T(8,128)} async-done(((f32[16,6144]{1,0:T(8,128)}), f32[64,6144]{1,0:T(8,128)}) %all-gather.72.cloned.1.call-update) | async-done | bytes 1572880 | tf_op jit(solution)/shard_map/all_gather | solution.py:22
  563.8 28.0 %all-gather.60.cloned.1.call-done = f32[64,1,6144]{2,1,0:T(1,128)} async-done(((f32[16,1,6144]{2,1,0:T(1,128)}), f32[64,1,6144]{2,1,0:T(1,128)}) %all-gather.60.cloned.1.call-update) | async-done | bytes 1572880 | tf_op jit(solution)/shard_map/all_gather | solution.py:22
  591.8 16.9 %all-gather.74.cloned.1.call-done = f32[128,6144]{1,0:T(8,128)} async-done(((f32[64,6144]{1,0:T(8,128)}), f32[128,6144]{1,0:T(8,128)}) %all-gather.74.cloned.1.call-update) | async-done | bytes 3145744 | tf_op jit(solution)/shard_map/all_gather | solution.py:22
  613.8 12.6 %all-gather.62.cloned.1.call-done = f32[128,1,6144]{2,1,0:T(1,128)} async-done(((f32[64,1,6144]{2,1,0:T(1,128)}), f32[128,1,6144]{2,1,0:T(1,128)}) %all-gather.62.cloned.1.call-update) | async-done | bytes 3145744 | tf_op jit(solution)/shard_map/all_gather | solution.py:22
  626.4 15.0 %fusion.28 = (f32[6144]{0:T(1024)S(1)}, f32[6144]{0:T(1024)S(1)}) fusion(f32[2,4,4,4,1,6144]{5,4,3,2,1,0:T(1,128)S(1)} %reshape.2692, pred[4,2,4,4]{0,2,3,1:T(4,128)(4,1)S(1)} %copy.251, f32[4,2,4,4,1,6144]{5,4,0,2,3,1:T(1,128)} %bitcast.469, pred[4,2,4,4]{0,2,3,1:T(4,128)(4,1)S(1)} %copy.249, pred[4,2,4,4]{0,2,3,1:T(4,128)(4,1)S(1)} %copy-done.8, ...), kind=kLoop, calls=%fused_computation.37 | loop fusion | flops 6279168 | bytes 6341120 | tf_op jit(solution)/shard_map/reduce_sum | solution.py:90
  (314 shorter events, 296.7 us)
Async XLA Ops:
  6.5 235.1 %all-gather.64.cloned.1.call-start = ((), (), s32[]{:S(2)}) async-start(), calls=%async_computation.6 | async-start | bytes 1966080 | tf_op jit(solution)/shard_map/all_gather | solution.py:22
  14.0 161.2 %copy-start.15 = (pred[8]{0:T(512)(128)(4,1)}, pred[8]{0:T(512)(128)(4,1)S(1)}, u32[]{:S(2)}) copy-start(pred[8]{0:T(512)(128)(4,1)S(1)} %iota_compare_fusion.1) | copy-start | bytes 28
  14.0 161.2 %copy-start.17 = (pred[8]{0:T(512)(128)(4,1)}, pred[8]{0:T(512)(128)(4,1)S(1)}, u32[]{:S(2)}) copy-start(pred[8]{0:T(512)(128)(4,1)S(1)} %iota_compare_fusion.3) | copy-start | bytes 28
  93.8 81.5 %copy-start.1 = (f32[768,8]{0,1:T(8,128)S(1)}, f32[768,8]{0,1:T(8,128)}, u32[]{:S(2)}) copy-start(f32[768,8]{0,1:T(8,128)} %param.5) | copy-start | bytes 73732
  189.6 24.6 %slice-start.4 = ((f32[8,768,8]{1,0,2:T(8,128)}), f32[1,768,8]{1,0,2:T(1,128)S(1)}, s32[]{:S(2)}) async-start(f32[8,768,8]{1,0,2:T(8,128)} %bitcast_subtract_fusion.2), calls=%async_computation.16 | async-start | bytes 49152 | tf_op jit(solution)/shard_map/slice | solution.py:70
  214.1 55.7 %all-gather.52.cloned.1.call-start = ((), (), s32[]{:S(2)}) async-start(), calls=%async_computation | async-start | bytes 1966080 | tf_op jit(solution)/shard_map/all_gather | solution.py:22
  234.6 52.1 %all-gather.66.cloned.1.call-start = ((), (), s32[]{:S(2)}) async-start(), calls=%async_computation.7 | async-start | bytes 4718592 | tf_op jit(solution)/shard_map/all_gather | solution.py:22
  241.6 62.8 %all-gather.54.cloned.1.call-start = ((), (), s32[]{:S(2)}) async-start(), calls=%async_computation.1 | async-start | bytes 4718592 | tf_op jit(solution)/shard_map/all_gather | solution.py:22
  269.8 133.0 %all-gather.68.cloned.1.call-start = ((), (), s32[]{:S(2)}) async-start(), calls=%async_computation.8 | async-start | bytes 1966080 | tf_op jit(solution)/shard_map/all_gather | solution.py:22
  270.7 33.8 %copy-start.6 = (pred[4,2,4,4]{0,2,3,1:T(4,128)(4,1)S(1)}, pred[4,2,4,4]{0,2,3,1:T(4,128)(4,1)}, u32[]{:S(2)}) copy-start(pred[4,2,4,4]{0,2,3,1:T(4,128)(4,1)} %copy-done.5) | copy-start | bytes 388
  270.7 33.8 %copy-start.10 = (pred[4,2,4,4]{0,2,3,1:T(4,128)(4,1)S(1)}, pred[4,2,4,4]{0,2,3,1:T(4,128)(4,1)}, u32[]{:S(2)}) copy-start(pred[4,2,4,4]{0,2,3,1:T(4,128)(4,1)} %copy-done.9) | copy-start | bytes 388
  346.6 24.6 %slice-start.5 = ((f32[8,768,8]{1,0,2:T(8,128)}), f32[1,768,8]{1,0,2:T(1,128)S(1)}, s32[]{:S(2)}) async-start(f32[8,768,8]{1,0,2:T(8,128)} %bitcast_subtract_fusion.1), calls=%async_computation.17 | async-start | bytes 49152 | tf_op jit(solution)/shard_map/slice | solution.py:70
  371.1 59.8 %all-gather.56.cloned.1.call-start = ((), (), s32[]{:S(2)}) async-start(), calls=%async_computation.2 | async-start | bytes 1966080 | tf_op jit(solution)/shard_map/all_gather | solution.py:22
  392.1 55.7 %all-gather.70.cloned.1.call-start = ((), (), s32[]{:S(2)}) async-start(), calls=%async_computation.9 | async-start | bytes 4718592 | tf_op jit(solution)/shard_map/all_gather | solution.py:22
  402.8 62.8 %all-gather.58.cloned.1.call-start = ((), (), s32[]{:S(2)}) async-start(), calls=%async_computation.3 | async-start | bytes 4718592 | tf_op jit(solution)/shard_map/all_gather | solution.py:22
  430.9 34.8 %copy-start.7 = (pred[4,2,4,4]{0,2,3,1:T(4,128)(4,1)S(1)}, pred[4,2,4,4]{0,2,3,1:T(4,128)(4,1)}, u32[]{:S(2)}) copy-start(pred[4,2,4,4]{0,2,3,1:T(4,128)(4,1)} %copy-done.5) | copy-start | bytes 388
  430.9 34.7 %copy-start.11 = (pred[4,2,4,4]{0,2,3,1:T(4,128)(4,1)S(1)}, pred[4,2,4,4]{0,2,3,1:T(4,128)(4,1)}, u32[]{:S(2)}) copy-start(pred[4,2,4,4]{0,2,3,1:T(4,128)(4,1)} %copy-done.9) | copy-start | bytes 388
  430.9 132.8 %all-gather.72.cloned.1.call-start = ((), (), s32[]{:S(2)}) async-start(), calls=%async_computation.10 | async-start | bytes 1966080 | tf_op jit(solution)/shard_map/all_gather | solution.py:22
  507.5 24.6 %slice-start.3 = ((f32[8,768,8]{1,0,2:T(8,128)}), f32[1,768,8]{1,0,2:T(1,128)S(1)}, s32[]{:S(2)}) async-start(f32[8,768,8]{1,0,2:T(8,128)} %bitcast_subtract_fusion), calls=%async_computation.15 | async-start | bytes 49152 | tf_op jit(solution)/shard_map/slice | solution.py:70
  532.0 59.8 %all-gather.60.cloned.1.call-start = ((), (), s32[]{:S(2)}) async-start(), calls=%async_computation.4 | async-start | bytes 1966080 | tf_op jit(solution)/shard_map/all_gather | solution.py:22
  553.0 55.7 %all-gather.74.cloned.1.call-start = ((), (), s32[]{:S(2)}) async-start(), calls=%async_computation.11 | async-start | bytes 4718592 | tf_op jit(solution)/shard_map/all_gather | solution.py:22
  563.8 62.7 %all-gather.62.cloned.1.call-start = ((), (), s32[]{:S(2)}) async-start(), calls=%async_computation.5 | async-start | bytes 4718592 | tf_op jit(solution)/shard_map/all_gather | solution.py:22
  591.8 34.6 %copy-start.8 = (pred[4,2,4,4]{0,2,3,1:T(4,128)(4,1)S(1)}, pred[4,2,4,4]{0,2,3,1:T(4,128)(4,1)}, u32[]{:S(2)}) copy-start(pred[4,2,4,4]{0,2,3,1:T(4,128)(4,1)} %copy-done.5) | copy-start | bytes 388
  591.8 34.6 %copy-start.12 = (pred[4,2,4,4]{0,2,3,1:T(4,128)(4,1)S(1)}, pred[4,2,4,4]{0,2,3,1:T(4,128)(4,1)}, u32[]{:S(2)}) copy-start(pred[4,2,4,4]{0,2,3,1:T(4,128)(4,1)} %copy-done.9) | copy-start | bytes 388
  (14 other events, 129.5 us)
Sparse Core Ops, SparseCore 0:
  214.3 27.3 all-gather.63
  243.3 26.4 all-gather.51
  271.5 15.2 all-gather.65
  288.2 16.1 all-gather.53
  371.2 31.5 all-gather.67
  404.3 26.4 all-gather.55
  432.5 15.2 all-gather.69
  449.4 16.1 all-gather.57
  532.1 31.5 all-gather.71
  565.2 26.4 all-gather.59
  593.4 15.2 all-gather.73
  610.2 16.1 all-gather.61
where the time goes:
time: 669 us; the launch traced here: 663 us
  blocking collectives  257 us (38%)
  waiting for transfers between devices  200 us (30%)
  other arithmetic  71.5 us (11%)
  matrix products  59.3 us (9%)
  local copies, waits for them, and re-layouts  52.6 us (8%)
  between operations  21.7 us (3%)
    all_gather x23, blocking collectives, gather_in_order(): blocks = lax.all_gather(blocks, axes[k], axis=0, tiled=True)  225 us
    all_gather x12, waiting for transfers between devices, gather_in_order(): blocks = lax.all_gather(blocks, axes[k], axis=0, tiled=True)  200 us
    reduce_sum x5, other arithmetic, settle(): jnp.sum(jnp.where(head_first, heads_all, 0.0) + jnp.where(tail_first, tai...  47.1 us
    dot_general x4, matrix products, lifted_terms(): spread = jnp.dot(block, flat_frames, preferred_element_type=jnp.float32)  35.1 us
    unnamed x4, blocking collectives  32 us
    reshape x8, local copies, waits for them, and re-layouts, gather_in_order(): blocks = blocks.reshape(*block, *value.shape)  16.1 us
    dot_general x3, matrix products, local_moment(): lax.dot_general(block, lifted.reshape(block.shape[0], -1), (((0,), (0,)),...  16 us
  transfers between devices with their start and end apart: 12, of which 12 were waited for; matrix products, arithmetic and copies ran while one was open for 3% of the time, Pallas kernels for 0%

commit v1 on v0

--- a/solution.py
+++ b/solution.py
@@ -19,7 +19,10 @@
 def gather_in_order(value, axes, order):
     blocks = value[None]
     for k in order:
-        blocks = lax.all_gather(blocks, axes[k], axis=0, tiled=True)
+        n_dev = lax.axis_size(axes[k])
+        parts = jnp.stack([blocks for _ in range(n_dev)])
+        parts = lax.all_to_all(parts, axes[k], split_axis=0, concat_axis=0)
+        blocks = jnp.concatenate(parts, axis=0)
     block = [lax.axis_size(axes[k]) for k in reversed(order)]
     blocks = blocks.reshape(*block, *value.shape)
     turned = sorted(range(len(order)), key=lambda place: order[len(order) - 1 - place])

time: 669 us -> 631 us (0.943)
  blocking collectives: 257 us -> 13.9 us
  starting transfers between devices: 0.66 us -> 192 us
  local copies, waits for them, and re-layouts: 52.6 us -> 93.4 us
  waiting for transfers between devices: 200 us -> 178 us
  between operations: 21.7 us -> 6.17 us
    all_gather x23 -> x0, blocking collectives: 225 us -> none  [gather_in_order(): blocks = lax.all_gather(blocks, axes[k], axis=0, tiled=True)]
    all_gather x12 -> x0, waiting for transfers between devices: 200 us -> none  [gather_in_order(): blocks = lax.all_gather(blocks, axes[k], axis=0, tiled=True)]
    all_to_all x0 -> x41, starting transfers between devices: none -> 192 us  [gather_in_order(): parts = lax.all_to_all(parts, axes[k], split_axis=0, concat_axis=0)]
    all_to_all x0 -> x41, waiting for transfers between devices: none -> 178 us  [gather_in_order(): parts = lax.all_to_all(parts, axes[k], split_axis=0, concat_axis=0)]
    unnamed x4 -> x0, blocking collectives: 32 us -> none
    another operation x0 -> x53, local copies, waits for them, and re-layouts: none -> 30.7 us  [the longest x50 30.4 us: gather_in_order(): parts = jnp.stack([blocks for _ in range(n_dev)])]
    all_to_all x0 -> x13, local copies, waits for them, and re-layouts: none -> 27.6 us  [gather_in_order(): parts = lax.all_to_all(parts, axes[k], split_axis=0, concat_axis=0)]
    reduce_sum x5, other arithmetic: 47.1 us -> 24.3 us  [settle(): jnp.sum(jnp.where(head_first, heads_all, 0.0) + jnp.where(tail_first, tai...]
  transfers between devices with their start and end apart: 12 -> 41, of which waited for: 12 -> 33; matrix products, arithmetic and copies ran while one was open for 3% -> 11% of each run, Pallas kernels for 0% -> 0%
where the time goes in v1:
time: 631 us; the launch traced here: 619 us
  starting transfers between devices  192 us (30%)
  waiting for transfers between devices  178 us (28%)
  local copies, waits for them, and re-layouts  93.4 us (15%)
  other arithmetic  71.1 us (11%)
  matrix products  63.7 us (10%)
  blocking collectives  13.9 us (2%)
    all_to_all x41, starting transfers between devices, gather_in_order(): parts = lax.all_to_all(parts, axes[k], split_axis=0, concat_axis=0)  192 us
    all_to_all x41, waiting for transfers between devices, gather_in_order(): parts = lax.all_to_all(parts, axes[k], split_axis=0, concat_axis=0)  178 us
    dot_general x4, matrix products, lifted_terms(): spread = jnp.dot(block, flat_frames, preferred_element_type=jnp.float32)  34.9 us
    another operation x50, local copies, waits for them, and re-layouts, gather_in_order(): parts = jnp.stack([blocks for _ in range(n_dev)])  30.4 us
    all_to_all x13, local copies, waits for them, and re-layouts, gather_in_order(): parts = lax.all_to_all(parts, axes[k], split_axis=0, concat_axis=0)  27.6 us
    reduce_sum x5, other arithmetic, settle(): jnp.sum(jnp.where(head_first, heads_all, 0.0) + jnp.where(tail_first, tai...  24.3 us
    dot_general x3, matrix products, local_moment(): lax.dot_general(block, lifted.reshape(block.shape[0], -1), (((0,), (0,)),...  20.6 us
    another operation x10, other arithmetic, gather_in_order(): parts = jnp.stack([blocks for _ in range(n_dev)])  20 us
  transfers between devices with their start and end apart: 41, of which 33 were waited for; matrix products, arithmetic and copies ran while one was open for 11% of the time, Pallas kernels for 0%

profile of v1, /device:TPU:1, one launch (start us, length us, event | category | flops | bytes accessed | tf_op | source)
XLA Modules:
  0.0 618.9 jit_solution(12283485943534989718)
XLA Ops:
  12.2 6.3 %fusion.64 = f32[8,768]{1,0:T(8,128)S(1)} fusion(bf16[8192,768]{1,0:T(8,128)(2,1)} %param.3, s32[8192]{0:T(1024)S(1)} %broadcast_subtract_fusion), kind=kOutput, calls=%fused_computation.340 | convolution fusion | flops 100859904 | bytes 12640256 | tf_op jit(solution)/shard_map/dot_general | solution.py:125
  86.0 14.5 %all-to-all-start.19 = ((f32[2,64,1,1]{1,3,2,0:T(1,128)}), f32[2,64,1,1]{1,3,2,0:T(1,128)S(1)}, u32[]{:S(2)}, u32[]{:S(2)}) async-start(f32[2,64,1,1]{1,3,2,0:T(1,128)} %pad_maximum_fusion.10), calls=%async_computation.19 | async-start | bytes 2048 | tf_op jit(solution)/shard_map/all_to_all | solution.py:24
  108.7 6.5 %all_to_all.234 = f32[4,1,1,768]{3,2,1,0:T(1,128)S(1)} all-to-all(f32[4,1,1,768]{3,2,1,0:T(1,128)S(1)} %stack.206), channel_id=1, replica_groups=mesh['row_0'=4,'row_1'=2,'col_0'=4,'col_1'=4] {'row_0'}, dimensions={0} | all-to-all | bytes 24576 | tf_op jit(solution)/shard_map/all_to_all | solution.py:24
  158.9 10.0 %all-to-all-start.11 = ((f32[2,64,1,768]{3,1,2,0:T(8,128)}), f32[2,64,1,768]{3,1,2,0:T(8,128)S(1)}, u32[]{:S(2)}, u32[]{:S(2)}) async-start(f32[2,64,1,768]{3,1,2,0:T(8,128)} %pad_maximum_fusion.7), calls=%async_computation.11 | async-start | bytes 786432 | tf_op jit(solution)/shard_map/all_to_all | solution.py:24
  177.0 8.6 %convert_reduce_fusion.2 = (f32[8,8]{1,0:T(8,128)S(1)}, bf16[8192,8,8]{0,2,1:T(8,128)(2,1)S(1)}) fusion(bf16[8192,8]{0,1:T(8,128)(2,1)S(1)} %get-tuple-element.187, f32[8,8]{1,0:T(8,128)S(1)} %bitcast.522, bf16[768,8]{0,1:T(8,128)(2,1)S(1)} %convert_element_type.75, bf16[8192,768]{1,0:T(8,128)(2,1)} %param.3), kind=kOutput, calls=%fused_computation.30 | convolution fusion | flops 807927744 | bytes 13775360 | tf_op jit(solution)/shard_map/dot_general | solution.py:50
  185.6 6.8 %convolution_bitcast_fusion.3 = f32[768,8,8]{0,2,1:T(8,128)S(1)} fusion(bf16[8192,768]{1,0:T(8,128)(2,1)} %param.3, bf16[8192,8,8]{0,2,1:T(8,128)(2,1)S(1)} %get-tuple-element.200), kind=kOutput, calls=%fused_computation.34 | convolution fusion | flops 805306368 | bytes 13828096 | tf_op jit(solution)/shard_map/dot_general | solution.py:57
  220.3 6.2 %all-to-all-done.21 = f32[4,4,1,6144]{3,1,2,0:T(4,128)S(1)} async-done(((f32[4,4,1,6144]{3,1,2,0:T(4,128)}), f32[4,4,1,6144]{3,1,2,0:T(4,128)S(1)}, u32[]{:S(2)}, u32[]{:S(2)}) %all-to-all-start.21) | async-done | bytes 393248 | tf_op jit(solution)/shard_map/all_to_all | solution.py:24
  242.0 15.1 %all-to-all-done.22 = f32[4,16,1,6144]{3,1,2,0:T(8,128)S(1)} async-done(((f32[4,16,1,6144]{3,1,2,0:T(8,128)}), f32[4,16,1,6144]{3,1,2,0:T(8,128)S(1)}, u32[]{:S(2)}, u32[]{:S(2)}) %all-to-all-start.22) | async-done | bytes 1572896 | tf_op jit(solution)/shard_map/all_to_all | solution.py:24
  263.9 12.1 %all-to-all-done.26 = f32[4,16,1,6144]{3,1,2,0:T(8,128)S(1)} async-done(((f32[4,16,1,6144]{3,1,2,0:T(8,128)}), f32[4,16,1,6144]{3,1,2,0:T(8,128)S(1)}, u32[]{:S(2)}, u32[]{:S(2)}) %all-to-all-start.26) | async-done | bytes 1572896 | tf_op jit(solution)/shard_map/all_to_all | solution.py:24
  277.1 11.5 %all-to-all-start.23 = ((f32[2,64,1,6144]{3,1,2,0:T(8,128)}), f32[2,64,1,6144]{3,1,2,0:T(8,128)S(1)}, u32[]{:S(2)}, u32[]{:S(2)}) async-start(f32[2,64,1,6144]{3,1,2,0:T(8,128)} %pad_maximum_fusion), calls=%async_computation.23 | async-start | bytes 6291456 | tf_op jit(solution)/shard_map/all_to_all | solution.py:24
  306.4 8.1 %add_reduce_fusion.5 = (f32[6144]{0:T(1024)}, f32[6144]{0:T(1024)}) fusion(f32[4,2,4,4,1,6144]{5,1,0,2,3,4:T(2,128)S(1)} %bitcast.491, f32[4,2,4,4,1,6144]{5,1,0,2,3,4:T(2,128)S(1)} %bitcast.488, pred[4,2,4,4]{1,0,2,3:T(4,128)(4,1)S(1)} %copy-done.19, pred[4,2,4,4]{1,0,2,3:T(4,128)(4,1)S(1)} %copy-done.15, pred[4,2,4,4]{1,0,2,3:T(4,128)(4,1)S(1)} %copy-done.23, ...), kind=kLoop, calls=%fused_computation.27 | loop fusion | flops 6279168 | bytes 6341120 | tf_op jit(solution)/shard_map/reduce_sum | solution.py:93
  322.3 8.6 %convert_reduce_fusion.1 = (f32[64]{0:T(128)S(1)}, bf16[8192,64]{0,1:T(8,128)(2,1)S(1)}) fusion(bf16[8192,8]{0,1:T(8,128)(2,1)S(1)} %get-tuple-element.187, f32[64]{0:T(128)S(1)} %sub.799, bf16[8192,768]{1,0:T(8,128)(2,1)} %param.3, bf16[768,8,8]{0,1,2:T(8,128)(2,1)S(1)} %convert_bitcast_fusion.2), kind=kOutput, calls=%fused_computation.29 | convolution fusion | flops 807927744 | bytes 13861376 | tf_op jit(solution)/shard_map/dot_general | solution.py:50
  331.1 6.9 %convolution_bitcast_fusion.2 = f32[768,8,8]{0,2,1:T(8,128)S(1)} fusion(bf16[8192,64]{0,1:T(8,128)(2,1)S(1)} %get-tuple-element.202, bf16[8192,768]{1,0:T(8,128)(2,1)} %param.3), kind=kOutput, calls=%fused_computation.33 | convolution fusion | flops 805306368 | bytes 13828096 | tf_op jit(solution)/shard_map/dot_general | solution.py:57
  386.8 15.8 %all-to-all-done.30 = f32[4,16,1,6144]{3,1,2,0:T(8,128)S(1)} async-done(((f32[4,16,1,6144]{3,1,2,0:T(8,128)}), f32[4,16,1,6144]{3,1,2,0:T(8,128)S(1)}, u32[]{:S(2)}, u32[]{:S(2)}) %all-to-all-start.30) | async-done | bytes 1572896 | tf_op jit(solution)/shard_map/all_to_all | solution.py:24
  409.4 12.8 %all-to-all-done.34 = f32[4,16,1,6144]{3,1,2,0:T(8,128)S(1)} async-done(((f32[4,16,1,6144]{3,1,2,0:T(8,128)}), f32[4,16,1,6144]{3,1,2,0:T(8,128)S(1)}, u32[]{:S(2)}, u32[]{:S(2)}) %all-to-all-start.34) | async-done | bytes 1572896 | tf_op jit(solution)/shard_map/all_to_all | solution.py:24
  423.3 10.8 %all-to-all-start.31 = ((f32[2,64,1,6144]{3,1,2,0:T(8,128)}), f32[2,64,1,6144]{3,1,2,0:T(8,128)S(1)}, u32[]{:S(2)}, u32[]{:S(2)}) async-start(f32[2,64,1,6144]{3,1,2,0:T(8,128)} %pad_maximum_fusion.2), calls=%async_computation.31 | async-start | bytes 6291456 | tf_op jit(solution)/shard_map/all_to_all | solution.py:24
  452.0 7.6 %add_reduce_fusion.3 = (f32[6144]{0:T(1024)}, f32[6144]{0:T(1024)}) fusion(f32[4,2,4,4,1,6144]{5,1,0,2,3,4:T(2,128)S(1)} %bitcast.492, f32[4,2,4,4,1,6144]{5,1,0,2,3,4:T(2,128)S(1)} %bitcast.489, pred[4,2,4,4]{1,0,2,3:T(4,128)(4,1)S(1)} %copy-done.20, pred[4,2,4,4]{1,0,2,3:T(4,128)(4,1)S(1)} %copy-done.16, pred[4,2,4,4]{1,0,2,3:T(4,128)(4,1)S(1)} %copy-done.24, ...), kind=kLoop, calls=%fused_computation.25 | loop fusion | flops 6279168 | bytes 6341120 | tf_op jit(solution)/shard_map/reduce_sum | solution.py:93
  467.4 8.6 %convert_reduce_fusion = (f32[64]{0:T(128)S(1)}, bf16[8192,64]{0,1:T(8,128)(2,1)S(1)}) fusion(bf16[8192,8]{0,1:T(8,128)(2,1)S(1)} %get-tuple-element.187, f32[64]{0:T(128)S(1)} %sub.859, bf16[8192,768]{1,0:T(8,128)(2,1)} %param.3, bf16[768,8,8]{0,1,2:T(8,128)(2,1)S(1)} %convert_bitcast_fusion.1), kind=kOutput, calls=%fused_computation.28 | convolution fusion | flops 807927744 | bytes 13861376 | tf_op jit(solution)/shard_map/dot_general | solution.py:50
  476.2 6.9 %convolution_bitcast_fusion.1 = f32[768,8,8]{0,2,1:T(8,128)S(1)} fusion(bf16[8192,64]{0,1:T(8,128)(2,1)S(1)} %get-tuple-element.204, bf16[8192,768]{1,0:T(8,128)(2,1)} %param.3), kind=kOutput, calls=%fused_computation.32 | convolution fusion | flops 805306368 | bytes 13828096 | tf_op jit(solution)/shard_map/dot_general | solution.py:57
  531.3 15.8 %all-to-all-done.38 = f32[4,16,1,6144]{3,1,2,0:T(8,128)S(1)} async-done(((f32[4,16,1,6144]{3,1,2,0:T(8,128)}), f32[4,16,1,6144]{3,1,2,0:T(8,128)S(1)}, u32[]{:S(2)}, u32[]{:S(2)}) %all-to-all-start.38) | async-done | bytes 1572896 | tf_op jit(solution)/shard_map/all_to_all | solution.py:24
  553.8 12.8 %all-to-all-done.42 = f32[4,16,1,6144]{3,1,2,0:T(8,128)S(1)} async-done(((f32[4,16,1,6144]{3,1,2,0:T(8,128)}), f32[4,16,1,6144]{3,1,2,0:T(8,128)S(1)}, u32[]{:S(2)}, u32[]{:S(2)}) %all-to-all-start.42) | async-done | bytes 1572896 | tf_op jit(solution)/shard_map/all_to_all | solution.py:24
  567.7 10.8 %all-to-all-start.39 = ((f32[2,64,1,6144]{3,1,2,0:T(8,128)}), f32[2,64,1,6144]{3,1,2,0:T(8,128)S(1)}, u32[]{:S(2)}, u32[]{:S(2)}) async-start(f32[2,64,1,6144]{3,1,2,0:T(8,128)} %pad_maximum_fusion.4), calls=%async_computation.39 | async-start | bytes 6291456 | tf_op jit(solution)/shard_map/all_to_all | solution.py:24
  596.4 7.2 %add_reduce_fusion.1 = (f32[6144]{0:T(1024)S(1)}, f32[6144]{0:T(1024)S(1)}) fusion(f32[4,2,4,4,1,6144]{5,1,0,2,3,4:T(2,128)S(1)} %bitcast.490, f32[4,2,4,4,1,6144]{5,1,0,2,3,4:T(2,128)S(1)} %bitcast.487, pred[4,2,4,4]{1,0,2,3:T(4,128)(4,1)S(1)} %copy-done.21, pred[4,2,4,4]{1,0,2,3:T(4,128)(4,1)S(1)} %copy-done.17, pred[4,2,4,4]{1,0,2,3:T(4,128)(4,1)S(1)} %copy-done.25, ...), kind=kLoop, calls=%fused_computation.23 | loop fusion | flops 6279168 | bytes 6341120 | tf_op jit(solution)/shard_map/reduce_sum | solution.py:93
  609.3 9.2 %fusion.19 = f32[8192,8]{0,1:T(8,128)} fusion(bf16[8192,768]{1,0:T(8,128)(2,1)} %param.3, f32[8192,8]{0,1:T(8,128)S(1)} %copy-done.6, f32[8,8]{1,0:T(8,128)S(1)} %bitcast.517, bf16[768,8,8]{0,1,2:T(8,128)(2,1)S(1)} %convert_bitcast_fusion), kind=kOutput, calls=%fused_computation.31 | convolution fusion | flops 806813696 | bytes 13205760 | tf_op jit(solution)/shard_map/dot_general | solution.py:50
  (409 shorter events, 373.7 us)
Async XLA Ops:
  6.0 12.7 %all-to-all-start.16 = ((f32[4,1,1,1]{3,2,1,0:T(1,128)}), f32[4,1,1,1]{3,2,1,0:T(1,128)S(1)}, u32[]{:S(2)}, u32[]{:S(2)}) async-start(f32[4,1,1,1]{3,2,1,0:T(1,128)} %stack.214), calls=%async_computation.16 | async-start | bytes 4096 | tf_op jit(solution)/shard_map/all_to_all | solution.py:24
  61.1 9.1 %all-to-all-start.18 = ((f32[4,16,1,1]{1,3,2,0:T(1,128)}), f32[4,16,1,1]{1,3,2,0:T(1,128)S(1)}, u32[]{:S(2)}, u32[]{:S(2)}) async-start(f32[4,16,1,1]{1,3,2,0:T(1,128)} %stack.216), calls=%async_computation.18 | async-start | bytes 4096 | tf_op jit(solution)/shard_map/all_to_all | solution.py:24
  86.0 15.4 %all-to-all-start.19 = ((f32[2,64,1,1]{1,3,2,0:T(1,128)}), f32[2,64,1,1]{1,3,2,0:T(1,128)S(1)}, u32[]{:S(2)}, u32[]{:S(2)}) async-start(f32[2,64,1,1]{1,3,2,0:T(1,128)} %pad_maximum_fusion.10), calls=%async_computation.19 | async-start | bytes 2048 | tf_op jit(solution)/shard_map/all_to_all | solution.py:24
  158.9 11.3 %all-to-all-start.11 = ((f32[2,64,1,768]{3,1,2,0:T(8,128)}), f32[2,64,1,768]{3,1,2,0:T(8,128)S(1)}, u32[]{:S(2)}, u32[]{:S(2)}) async-start(f32[2,64,1,768]{3,1,2,0:T(8,128)} %pad_maximum_fusion.7), calls=%async_computation.11 | async-start | bytes 786432 | tf_op jit(solution)/shard_map/all_to_all | solution.py:24
  198.0 8.8 %all-to-all-start.20 = ((f32[4,1,1,6144]{3,2,1,0:T(1,128)}), f32[4,1,1,6144]{3,2,1,0:T(1,128)}, u32[]{:S(2)}, u32[]{:S(2)}) async-start(f32[4,1,1,6144]{3,2,1,0:T(1,128)} %stack.218), calls=%async_computation.20 | async-start | bytes 196608 | tf_op jit(solution)/shard_map/all_to_all | solution.py:24
  216.2 10.3 %all-to-all-start.21 = ((f32[4,4,1,6144]{3,1,2,0:T(4,128)}), f32[4,4,1,6144]{3,1,2,0:T(4,128)S(1)}, u32[]{:S(2)}, u32[]{:S(2)}) async-start(f32[4,4,1,6144]{3,1,2,0:T(4,128)} %stack.219), calls=%async_computation.21 | async-start | bytes 786432 | tf_op jit(solution)/shard_map/all_to_all | solution.py:24
  227.3 9.7 %all-to-all-start.25 = ((f32[4,4,1,6144]{3,1,2,0:T(4,128)}), f32[4,4,1,6144]{3,1,2,0:T(4,128)S(1)}, u32[]{:S(2)}, u32[]{:S(2)}) async-start(f32[4,4,1,6144]{3,1,2,0:T(4,128)} %stack.223), calls=%async_computation.25 | async-start | bytes 786432 | tf_op jit(solution)/shard_map/all_to_all | solution.py:24
  238.2 18.8 %all-to-all-start.22 = ((f32[4,16,1,6144]{3,1,2,0:T(8,128)}), f32[4,16,1,6144]{3,1,2,0:T(8,128)S(1)}, u32[]{:S(2)}, u32[]{:S(2)}) async-start(f32[4,16,1,6144]{3,1,2,0:T(8,128)} %stack.220), calls=%async_computation.22 | async-start | bytes 3145728 | tf_op jit(solution)/shard_map/all_to_all | solution.py:24
  258.3 17.6 %all-to-all-start.26 = ((f32[4,16,1,6144]{3,1,2,0:T(8,128)}), f32[4,16,1,6144]{3,1,2,0:T(8,128)S(1)}, u32[]{:S(2)}, u32[]{:S(2)}) async-start(f32[4,16,1,6144]{3,1,2,0:T(8,128)} %stack.224), calls=%async_computation.26 | async-start | bytes 3145728 | tf_op jit(solution)/shard_map/all_to_all | solution.py:24
  277.1 15.4 %all-to-all-start.23 = ((f32[2,64,1,6144]{3,1,2,0:T(8,128)}), f32[2,64,1,6144]{3,1,2,0:T(8,128)S(1)}, u32[]{:S(2)}, u32[]{:S(2)}) async-start(f32[2,64,1,6144]{3,1,2,0:T(8,128)} %pad_maximum_fusion), calls=%async_computation.23 | async-start | bytes 6291456 | tf_op jit(solution)/shard_map/all_to_all | solution.py:24
  292.5 9.4 %all-to-all-start.27 = ((f32[2,64,1,6144]{3,1,2,0:T(8,128)}), f32[2,64,1,6144]{3,1,2,0:T(8,128)}, u32[]{:S(2)}, u32[]{:S(2)}) async-start(f32[2,64,1,6144]{3,1,2,0:T(8,128)} %pad_maximum_fusion.1), calls=%async_computation.27 | async-start | bytes 6291456 | tf_op jit(solution)/shard_map/all_to_all | solution.py:24
  343.5 8.7 %all-to-all-start.28 = ((f32[4,1,1,6144]{3,2,1,0:T(1,128)}), f32[4,1,1,6144]{3,2,1,0:T(1,128)}, u32[]{:S(2)}, u32[]{:S(2)}) async-start(f32[4,1,1,6144]{3,2,1,0:T(1,128)} %stack.227), calls=%async_computation.28 | async-start | bytes 196608 | tf_op jit(solution)/shard_map/all_to_all | solution.py:24
  361.6 9.7 %all-to-all-start.29 = ((f32[4,4,1,6144]{3,1,2,0:T(4,128)}), f32[4,4,1,6144]{3,1,2,0:T(4,128)S(1)}, u32[]{:S(2)}, u32[]{:S(2)}) async-start(f32[4,4,1,6144]{3,1,2,0:T(4,128)} %stack.228), calls=%async_computation.29 | async-start | bytes 786432 | tf_op jit(solution)/shard_map/all_to_all | solution.py:24
  372.0 9.7 %all-to-all-start.33 = ((f32[4,4,1,6144]{3,1,2,0:T(4,128)}), f32[4,4,1,6144]{3,1,2,0:T(4,128)S(1)}, u32[]{:S(2)}, u32[]{:S(2)}) async-start(f32[4,4,1,6144]{3,1,2,0:T(4,128)} %stack.232), calls=%async_computation.33 | async-start | bytes 786432 | tf_op jit(solution)/shard_map/all_to_all | solution.py:24
  383.0 19.6 %all-to-all-start.30 = ((f32[4,16,1,6144]{3,1,2,0:T(8,128)}), f32[4,16,1,6144]{3,1,2,0:T(8,128)S(1)}, u32[]{:S(2)}, u32[]{:S(2)}) async-start(f32[4,16,1,6144]{3,1,2,0:T(8,128)} %stack.229), calls=%async_computation.30 | async-start | bytes 3145728 | tf_op jit(solution)/shard_map/all_to_all | solution.py:24
  403.9 18.3 %all-to-all-start.34 = ((f32[4,16,1,6144]{3,1,2,0:T(8,128)}), f32[4,16,1,6144]{3,1,2,0:T(8,128)S(1)}, u32[]{:S(2)}, u32[]{:S(2)}) async-start(f32[4,16,1,6144]{3,1,2,0:T(8,128)} %stack.233), calls=%async_computation.34 | async-start | bytes 3145728 | tf_op jit(solution)/shard_map/all_to_all | solution.py:24
  423.3 14.7 %all-to-all-start.31 = ((f32[2,64,1,6144]{3,1,2,0:T(8,128)}), f32[2,64,1,6144]{3,1,2,0:T(8,128)S(1)}, u32[]{:S(2)}, u32[]{:S(2)}) async-start(f32[2,64,1,6144]{3,1,2,0:T(8,128)} %pad_maximum_fusion.2), calls=%async_computation.31 | async-start | bytes 6291456 | tf_op jit(solution)/shard_map/all_to_all | solution.py:24
  438.1 9.4 %all-to-all-start.35 = ((f32[2,64,1,6144]{3,1,2,0:T(8,128)}), f32[2,64,1,6144]{3,1,2,0:T(8,128)}, u32[]{:S(2)}, u32[]{:S(2)}) async-start(f32[2,64,1,6144]{3,1,2,0:T(8,128)} %pad_maximum_fusion.3), calls=%async_computation.35 | async-start | bytes 6291456 | tf_op jit(solution)/shard_map/all_to_all | solution.py:24
  506.0 9.7 %all-to-all-start.37 = ((f32[4,4,1,6144]{3,1,2,0:T(4,128)}), f32[4,4,1,6144]{3,1,2,0:T(4,128)S(1)}, u32[]{:S(2)}, u32[]{:S(2)}) async-start(f32[4,4,1,6144]{3,1,2,0:T(4,128)} %stack.237), calls=%async_computation.37 | async-start | bytes 786432 | tf_op jit(solution)/shard_map/all_to_all | solution.py:24
  516.4 9.7 %all-to-all-start.41 = ((f32[4,4,1,6144]{3,1,2,0:T(4,128)}), f32[4,4,1,6144]{3,1,2,0:T(4,128)S(1)}, u32[]{:S(2)}, u32[]{:S(2)}) async-start(f32[4,4,1,6144]{3,1,2,0:T(4,128)} %stack.241), calls=%async_computation.41 | async-start | bytes 786432 | tf_op jit(solution)/shard_map/all_to_all | solution.py:24
  527.3 19.7 %all-to-all-start.38 = ((f32[4,16,1,6144]{3,1,2,0:T(8,128)}), f32[4,16,1,6144]{3,1,2,0:T(8,128)S(1)}, u32[]{:S(2)}, u32[]{:S(2)}) async-start(f32[4,16,1,6144]{3,1,2,0:T(8,128)} %stack.238), calls=%async_computation.38 | async-start | bytes 3145728 | tf_op jit(solution)/shard_map/all_to_all | solution.py:24
  548.3 18.3 %all-to-all-start.42 = ((f32[4,16,1,6144]{3,1,2,0:T(8,128)}), f32[4,16,1,6144]{3,1,2,0:T(8,128)S(1)}, u32[]{:S(2)}, u32[]{:S(2)}) async-start(f32[4,16,1,6144]{3,1,2,0:T(8,128)} %stack.242), calls=%async_computation.42 | async-start | bytes 3145728 | tf_op jit(solution)/shard_map/all_to_all | solution.py:24
  567.7 14.7 %all-to-all-start.39 = ((f32[2,64,1,6144]{3,1,2,0:T(8,128)}), f32[2,64,1,6144]{3,1,2,0:T(8,128)S(1)}, u32[]{:S(2)}, u32[]{:S(2)}) async-start(f32[2,64,1,6144]{3,1,2,0:T(8,128)} %pad_maximum_fusion.4), calls=%async_computation.39 | async-start | bytes 6291456 | tf_op jit(solution)/shard_map/all_to_all | solution.py:24
  582.5 9.4 %all-to-all-start.43 = ((f32[2,64,1,6144]{3,1,2,0:T(8,128)}), f32[2,64,1,6144]{3,1,2,0:T(8,128)}, u32[]{:S(2)}, u32[]{:S(2)}) async-start(f32[2,64,1,6144]{3,1,2,0:T(8,128)} %pad_maximum_fusion.5), calls=%async_computation.43 | async-start | bytes 6291456 | tf_op jit(solution)/shard_map/all_to_all | solution.py:24
  (53 other events, 565.1 us)
